TPU v7x, 32 devices: a whole 2x2x4 slice. The times are simulated.
32 devices in a mesh: mem: 4 (over y, x), reg: 8 (over z, core).
Axes of the slice: x: 2, y: 2, z: 4, core: 2. Of those that a mesh axis runs over, the one named last changes fastest.
Arguments:
- alpha: float32 [32, 16, 32, 128], P('mem', None, 'reg'), may hold values from -6 to 6
- perturbation: bfloat16 [32, 2, 16, 128, 512], P('mem', None, None, 'reg'), may hold values from -6 to 6
- obs_cell: int32 [8192], P('reg'), may hold values from 0 to 131071
- obs_kind: int32 [8192], P('reg'), may hold values from 0 to 3
- obs_value: float32 [8192], P('reg'), may hold values from -6 to 6
- obs_weight: float32 [8192], P('reg'), may hold values from 1 to 4
Outputs:
- obs_gradient: float32 [32, 16, 32, 128], P('mem', None, 'reg')
Inputs may be any that keep to these rules, and one draw needn't show every extreme that they name: `obs_cell`: each entry is level * 16 * 512 + row * 512 + column of a fine cell, the row counted from the first row of the observation's own region. `obs_kind`: 0 zonal wind, 1 meridional wind, 2 relative vorticity, 3 zonal wind advection.
All inputs are finite; a program needn't handle non-finite values.
Results may differ from a plain program's by a relative error of at most 0.0003.
Values sent between devices are 32-bit elements; how exact they have to be, the bound alone decides.
No kernel may reach another device: no remote copies, remote signals or barrier semaphores. Data moves between devices by JAX's collectives and lax.ppermute only.
A program may use at most 64 MiB of HBM per device.

v0:
```python
import math
import jax
import jax.numpy as jnp
from jax import lax
from jax.sharding import PartitionSpec as P

PASSES = 2
diffuse = 0.2
highest = lax.Precision.HIGHEST


def padded_2(value, sides, width):
    for axis, dim in sides:
        devices, length = (lax.axis_size(axis), value.shape[dim])
        up = [(i, (i + 1) % devices) for i in range(devices - 1)]
        down = [(j, i) for i, j in up]
        last = lax.slice_in_dim(value, length - width, length, axis=dim)
        first = lax.slice_in_dim(value, 0, width, axis=dim)
        before = lax.ppermute(last, axis, up)
        after = lax.ppermute(first, axis, down)
        value = jnp.concatenate([before, value, after], axis=dim)
    return value


def from_behind(value, axis, by):
    devices = lax.axis_size(axis)
    pairs = [(i, i + by) for i in range(devices) if 0 <= i + by < devices]
    return lax.ppermute(value, axis, pairs)


def weights(fine_rows, fine_start, coarse_count, coarse_start):
    finer = (jnp.arange(fine_rows) + fine_start).astype(jnp.float32)
    coarser = (jnp.arange(coarse_count) + coarse_start).astype(jnp.float32)
    where_at = (finer[:, None] + 0.5) / 4.0 - 0.5
    return jnp.maximum(0.0, 1.0 - jnp.abs(where_at - coarser[None, :]))


def one_pass(block):
    padded = jnp.pad(block, ((0, 0), (0, 0), (1, 1), (1, 1)))
    beside_all = (
        padded[:, :, 2:, 1:-1]
        + padded[:, :, :-2, 1:-1]
        + padded[:, :, 1:-1, 2:]
        + padded[:, :, 1:-1, :-2]
    )
    return block + diffuse * (beside_all - 4.0 * block)


def slopes(padded):
    along_x = (padded[..., 2:, 1:-1] - padded[..., :-2, 1:-1]) * 0.5
    along_y = (padded[..., 1:-1, 2:] - padded[..., 1:-1, :-2]) * 0.5
    return (along_x, along_y)


def mask_rows(block, first_row, total_rows):
    rows_here = first_row + jnp.arange(block.shape[2])
    keeping = (rows_here >= 0) & (rows_here < total_rows)
    return jnp.where(keeping[None, None, :, None], block, 0.0)


def smooth_rows(block, passes, keep):
    region = lax.axis_index("reg")
    total_rows = block.shape[2] * lax.axis_size("reg")
    extended = padded_2(block, (("reg", 2),), passes + keep)
    first_row = region * block.shape[2] - passes - keep
    for step in range(passes):
        extended = one_pass(extended)[:, :, 1:-1, :]
        first_row = first_row + 1
        extended = mask_rows(extended, first_row, total_rows)
    return extended


def observe(extended, level_first, obs_cell, obs_kind, obs_value, obs_weight, back_rim):
    levels = extended.shape[1]
    rows = extended.shape[2] - 2
    fine_cols = extended.shape[3] - 2
    zonal_x, zonal_y = slopes(extended[0])
    merid_x, _ = slopes(extended[1])
    zonal = extended[0, :, 1:-1, 1:-1]
    merid = extended[1, :, 1:-1, 1:-1]
    fields = jnp.stack([zonal, merid, merid_x - zonal_y, zonal * zonal_x + merid * zonal_y])
    plane = rows * fine_cols
    level = obs_cell // plane
    rest = obs_cell % plane
    row_in = rest // fine_cols
    column = rest % fine_cols
    inside = (level >= level_first) & (level < level_first + levels)
    local_level = jnp.clip(level - level_first, 0, levels - 1)
    line_count = 4 * levels * rows
    line = obs_kind * (levels * rows) + local_level * rows + row_in
    line_hot = (line[:, None] == jnp.arange(line_count, dtype=jnp.int32)[None, :]).astype(
        jnp.float32
    )
    column_hot = (column[:, None] == jnp.arange(fine_cols, dtype=jnp.int32)[None, :]).astype(
        jnp.float32
    )
    table = fields.reshape(line_count, fine_cols)
    picked = jnp.dot(line_hot, table, precision=highest, preferred_element_type=jnp.float32)
    seen = jnp.sum(picked * column_hot, axis=1)
    misfit = jnp.where(inside, obs_weight * (seen - obs_value), 0.0)
    weighted = misfit[:, None] * column_hot
    adjoint = lax.dot_general(
        line_hot,
        weighted,
        (((0,), (0,)), ((), ())),
        precision=highest,
        preferred_element_type=jnp.float32,
    )
    adjoint = adjoint.reshape(4, levels, rows, fine_cols)
    back = back_rim(jnp.stack([adjoint[2], adjoint[3] * zonal, adjoint[3] * merid]))
    vort_x, vort_y = slopes(back[0])
    flux_x, _ = slopes(back[1])
    _, flux_y = slopes(back[2])
    grad_u = adjoint[0] + adjoint[3] * zonal_x + vort_y - flux_x - flux_y
    grad_v = adjoint[1] + adjoint[3] * zonal_y - vort_x
    return jnp.stack([grad_u, grad_v])


def local(alpha, perturbation, obs_cell, obs_kind, obs_value, obs_weight):
    members, levels, coarse_rows, coarse_cols = alpha.shape
    fine_rows = perturbation.shape[3]
    region = lax.axis_index("reg")
    scale = 1.0 / math.sqrt(members * lax.axis_size("mem"))
    rows_x = weights(fine_rows, region * fine_rows, coarse_rows + 2, region * coarse_rows - 1)
    rows_y = weights(perturbation.shape[4], 0, coarse_cols, 0)
    smoothed = smooth_rows(alpha, PASSES, 1)
    part = jnp.einsum("ia,mlab->mlib", rows_x, smoothed, precision=highest)
    fine = jnp.einsum("mlib,jb->mlij", part, rows_y, precision=highest)
    partial_value = jnp.sum(fine[:, None] * perturbation.astype(jnp.float32), axis=0) * scale
    whole = lax.psum(partial_value, "mem")
    level_first = 0
    extended = jnp.pad(padded_2(whole, (("reg", 2),), 1), ((0, 0), (0, 0), (0, 0), (1, 1)))

    def back_rim(carried):
        rimmed_rows = padded_2(carried, (("reg", 2),), 1)
        return jnp.pad(rimmed_rows, ((0, 0), (0, 0), (0, 0), (1, 1)))

    grad_fine = observe(extended, level_first, obs_cell, obs_kind, obs_value, obs_weight, back_rim)
    product = jnp.sum(perturbation.astype(jnp.float32) * grad_fine[None], axis=1)
    projected_part = jnp.einsum("mlij,jb->mlib", product, rows_y, precision=highest)
    coarse = jnp.einsum("ia,mlib->mlab", rows_x, projected_part, precision=highest) * scale
    from_above = from_behind(coarse[:, :, 0], "reg", -1)
    from_below = from_behind(coarse[:, :, -1], "reg", 1)
    inner = coarse[:, :, 1:-1]
    inner = inner.at[:, :, -1].add(from_above)
    inner = inner.at[:, :, 0].add(from_below)
    return smooth_rows(inner, PASSES, 0)


def solution(mesh):
    return jax.shard_map(
        local,
        mesh=mesh,
        in_specs=(
            P("mem", None, "reg", None),
            P("mem", None, None, "reg", None),
            P("reg"),
            P("reg"),
            P("reg"),
            P("reg"),
        ),
        out_specs=P("mem", None, "reg", None),
        check_vma=False,
    )
```

profile of v0, /device:TPU:1, one launch (start us, length us, event | category | flops | bytes accessed | tf_op | source)
XLA Modules:
  0.0 147.5 jit_solution(11208299931560446973)
XLA Ops:
  6.5 1.2 fusion.90
  7.7 4.6 %collective-permute-start = (f32[8,16,3,128]{3,1,0,2:T(8,128)S(1)}, f32[8,16,3,128]{3,1,0,2:T(8,128)S(1)}, u32[]{:S(2)}, u32[]{:S(2)}) collective-permute-start(f32[8,16,3,128]{3,1,0,2:T(8,128)S(1)} %copy.30), channel_id=1, source_target_pairs={{0,1},{1,2},{2,3},{3,4},{4,5},{5,6},{6,7},{8,9},{9,10},{10,11},{11... | collective-permute-start | bytes 589832 | tf_op jit(solution)/shard_map/ppermute | solution.py:19
  12.4 1.9 %collective-permute-start.1 = (f32[8,16,3,128]{3,1,0,2:T(8,128)S(1)}, f32[8,16,3,128]{3,1,0,2:T(8,128)S(1)}, u32[]{:S(2)}, u32[]{:S(2)}) collective-permute-start(f32[8,16,3,128]{3,1,0,2:T(8,128)S(1)} %copy.31), channel_id=1, source_target_pairs={{1,0},{2,1},{3,2},{4,3},{5,4},{6,5},{7,6},{9,8},{10,9},{11,10},{12... | collective-permute-start | bytes 589832 | tf_op jit(solution)/shard_map/ppermute | solution.py:20
  15.0 4.4 %collective-permute-done.1 = f32[8,16,3,128]{3,1,0,2:T(8,128)S(1)} collective-permute-done((f32[8,16,3,128]{3,1,0,2:T(8,128)S(1)}, f32[8,16,3,128]{3,1,0,2:T(8,128)S(1)}, u32[]{:S(2)}, u32[]{:S(2)}) %collective-permute-start.1) | collective-permute-done | bytes 196640 | tf_op jit(solution)/shard_map/ppermute | solution.py:20
  20.6 1.2 convolution_bitcast_fusion
  21.8 3.5 %fusion.49 = f32[8,16,16,512]{3,2,1,0:T(8,128)S(1)} fusion(f32[8,16,16,128]{3,2,1,0:T(8,128)S(1)} %convolution_bitcast_fusion, f32[128]{0:T(128)S(1)} %iota_convert_fusion, f32[512]{0:T(512)S(1)} %multiply_add_fusion), kind=kOutput, calls=%fused_computation.114 | convolution fusion | flops 1610874880 | bytes 5245440 | tf_op jit(solution)/shard_map/mlib,jb->mlij/dot_general | solution.py:128
  25.3 1.1 fusion
  26.5 1.1 broadcast_multiply_fusion
  27.6 52.2 %all-reduce.8.cloned.1.call-done = f32[2,16,16,512]{3,2,1,0:T(8,128)} async-done(((f32[2,16,16,512]{3,2,1,0:T(8,128)}), f32[2,16,16,512]{3,2,1,0:T(8,128)}) %all-reduce.8.cloned.1.call-update) | async-done | bytes 1048592 | tf_op jit(solution)/shard_map/psum | solution.py:130
  79.8 1.3 fusion.87
  81.1 3.8 %collective-permute-start.2 = (f32[2,16,1,512]{3,2,1,0:T(1,128)S(1)}, f32[2,16,1,512]{3,2,1,0:T(1,128)S(1)}, u32[]{:S(2)}, u32[]{:S(2)}) collective-permute-start(f32[2,16,1,512]{3,2,1,0:T(1,128)S(1)} %get-tuple-element.44), channel_id=1, source_target_pairs={{0,1},{1,2},{2,3},{3,4},{4,5},{5,6},{6,7},{8,9},{9,10},{10,11},{11... | collective-permute-start | bytes 196616 | tf_op jit(solution)/shard_map/ppermute | solution.py:19
  85.0 2.1 %collective-permute-start.3 = (f32[2,16,1,512]{3,2,1,0:T(1,128)S(1)}, f32[2,16,1,512]{3,2,1,0:T(1,128)S(1)}, u32[]{:S(2)}, u32[]{:S(2)}) collective-permute-start(f32[2,16,1,512]{3,2,1,0:T(1,128)S(1)} %get-tuple-element.45), channel_id=1, source_target_pairs={{1,0},{2,1},{3,2},{4,3},{5,4},{6,5},{7,6},{9,8},{10,9},{11,10},{12... | collective-permute-start | bytes 196616 | tf_op jit(solution)/shard_map/ppermute | solution.py:20
  87.2 3.4 %collective-permute-done.3 = f32[2,16,1,512]{3,2,1,0:T(1,128)S(1)} collective-permute-done((f32[2,16,1,512]{3,2,1,0:T(1,128)S(1)}, f32[2,16,1,512]{3,2,1,0:T(1,128)S(1)}, u32[]{:S(2)}, u32[]{:S(2)}) %collective-permute-start.3) | collective-permute-done | bytes 65568 | tf_op jit(solution)/shard_map/ppermute | solution.py:20
  90.6 2.3 %select_maximum_fusion.4 = f32[2,16,18,514]{3,2,1,0:T(8,128)S(1)} fusion(f32[2,16,1,512]{3,2,1,0:T(1,128)S(1)} %collective-permute-done.3, f32[2,16,16,512]{3,2,1,0:T(8,128)} %all-reduce.8.cloned.1.call-done, f32[2,16,1,512]{3,2,1,0:T(1,128)S(1)} %collective-permute-done.2), kind=kLoop, calls=%fused_computation.34 | loop fusion | flops 2368512 | bytes 2363904 | tf_op jit(solution)/shard_map/concatenate | solution.py:21
  93.0 1.1 copy-done
  94.1 0.8 fusion.27
  95.2 3.7 %select_reduce_fusion = f32[1024]{0:T(1024)S(1)} fusion(f32[1024,512]{1,0:T(8,128)S(1)} %bitcast.71, s32[1024]{0:T(1024)S(1)} %get-tuple-element.72, s32[1024]{0:T(1024)S(1)} %get-tuple-element.71), kind=kOutput, calls=%fused_computation.30 | convolution fusion | flops 6445071360 | bytes 2109440 | tf_op jit(solution)/shard_map/dot_general | solution.py:98
  98.8 4.2 %fusion.2 = f32[1024,512]{1,0:T(8,128)S(1)} fusion(s32[1024]{0:T(1024)S(1)} %get-tuple-element.72, f32[1024]{0:T(1024)S(1)} %multiply_select_fusion, s32[1024]{0:T(1024)S(1)} %get-tuple-element.71), kind=kOutput, calls=%fused_computation.7 | convolution fusion | flops 6444548096 | bytes 2109440 | tf_op jit(solution)/shard_map/dot_general | solution.py:102
  103.7 1.9 %collective-permute-start.4 = (f32[3,16,1,512]{3,2,1,0:T(1,128)S(1)}, f32[3,16,1,512]{3,2,1,0:T(1,128)S(1)}, u32[]{:S(2)}, u32[]{:S(2)}) collective-permute-start(f32[3,16,1,512]{3,2,1,0:T(1,128)S(1)} %get-tuple-element.40), channel_id=1, source_target_pairs={{0,1},{1,2},{2,3},{3,4},{4,5},{5,6},{6,7},{8,9},{9,10},{10,11},{11... | collective-permute-start | bytes 294920 | tf_op jit(solution)/shard_map/ppermute | solution.py:19
  105.6 2.6 %collective-permute-start.5 = (f32[3,16,1,512]{3,2,1,0:T(1,128)S(1)}, f32[3,16,1,512]{3,2,1,0:T(1,128)S(1)}, u32[]{:S(2)}, u32[]{:S(2)}) collective-permute-start(f32[3,16,1,512]{3,2,1,0:T(1,128)S(1)} %get-tuple-element.41), channel_id=1, source_target_pairs={{1,0},{2,1},{3,2},{4,3},{5,4},{6,5},{7,6},{9,8},{10,9},{11,10},{12... | collective-permute-start | bytes 294920 | tf_op jit(solution)/shard_map/ppermute | solution.py:20
  108.2 3.3 %collective-permute-done.5 = f32[3,16,1,512]{3,2,1,0:T(1,128)S(1)} collective-permute-done((f32[3,16,1,512]{3,2,1,0:T(1,128)S(1)}, f32[3,16,1,512]{3,2,1,0:T(1,128)S(1)}, u32[]{:S(2)}, u32[]{:S(2)}) %collective-permute-start.5) | collective-permute-done | bytes 98336 | tf_op jit(solution)/shard_map/ppermute | solution.py:20
  111.5 1.6 %select_maximum_fusion = f32[3,16,18,514]{3,2,1,0:T(8,128)S(1)} fusion(f32[3,16,1,512]{3,2,1,0:T(1,128)S(1)} %collective-permute-done.5, f32[3,16,1,512]{3,2,1,0:T(1,128)S(1)} %collective-permute-done.4, f32[1,16,16,512]{3,2,1,0:T(8,128)S(1)} %get-tuple-element.43, f32[1,16,16,512]{3,2,1,0:T(8,128)S(1)} %get-tuple-element.42, f32[1,16,16,512]{3,2,1,0:T(8,128)S(1)} %bitcast.70), kind=kLoop, calls=%fused_computation.9 | loop fusion | flops 5329152 | bytes 3545856 | tf_op jit(solution)/shard_map/concatenate | solution.py:21
  113.3 1.5 %fusion.18 = (f32[1,16,16,512]{3,2,1,0:T(8,128)S(1)}, f32[1,16,16,512]{3,2,1,0:T(8,128)S(1)}) fusion(f32[16,18,514]{2,1,0:T(8,128)S(1)} %get-tuple-element.31, f32[16,18,514]{2,1,0:T(8,128)S(1)} %get-tuple-element.29, f32[16,18,514]{2,1,0:T(8,128)S(1)} %get-tuple-element.30, f32[16,16,512]{2,1,0:T(8,128)S(1)} %bitcast.72, f32[16,16,512]{2,1,0:T(8,128)S(1)} %bitcast.68, ...), kind=kLoop, calls=%fused_computation.60 | loop fusion | flops 2621440 | bytes 8912896 | tf_op jit(solution)/shard_map/stack | solution.py:116
  115.5 1.2 fusion.1
  116.7 3.6 %fusion.47 = f32[8,16,16,128]{3,2,1,0:T(8,128)S(1)} fusion(f32[8,16,16,512]{3,2,1,0:T(8,128)S(1)} %fusion.1, f32[128]{0:T(128)S(1)} %iota_convert_fusion, f32[512]{0:T(512)S(1)} %multiply_add_fusion), kind=kOutput, calls=%fused_computation.112 | convolution fusion | flops 1610874880 | bytes 5245440 | tf_op jit(solution)/shard_map/mlij,jb->mlib/dot_general | solution.py:140
  121.2 1.9 %collective-permute-start.6 = (f32[8,16,128]{2,1,0:T(8,128)S(1)}, f32[8,16,128]{2,1,0:T(8,128)S(1)}, u32[]{:S(2)}, u32[]{:S(2)}) collective-permute-start(f32[8,16,128]{2,1,0:T(8,128)S(1)} %bitcast.76), channel_id=1, source_target_pairs={{1,0},{2,1},{3,2},{4,3},{5,4},{6,5},{7,6},{9,8},{10,9},{11,10},{12... | collective-permute-start | bytes 196616 | tf_op jit(solution)/shard_map/ppermute | solution.py:28
  123.2 3.6 %collective-permute-start.7 = (f32[8,16,128]{2,1,0:T(8,128)S(1)}, f32[8,16,128]{2,1,0:T(8,128)S(1)}, u32[]{:S(2)}, u32[]{:S(2)}) collective-permute-start(f32[8,16,128]{2,1,0:T(8,128)S(1)} %bitcast.75), channel_id=1, source_target_pairs={{0,1},{1,2},{2,3},{3,4},{4,5},{5,6},{6,7},{8,9},{9,10},{10,11},{11... | collective-permute-start | bytes 196616 | tf_op jit(solution)/shard_map/ppermute | solution.py:28
  126.9 1.3 collective-permute-done.7
  128.2 4.3 %collective-permute-start.8 = (f32[8,16,2,128]{3,1,0,2:T(8,128)S(1)}, f32[8,16,2,128]{3,1,0,2:T(8,128)S(1)}, u32[]{:S(2)}, u32[]{:S(2)}) collective-permute-start(f32[8,16,2,128]{3,1,0,2:T(8,128)S(1)} %get-tuple-element.67), channel_id=1, source_target_pairs={{0,1},{1,2},{2,3},{3,4},{4,5},{5,6},{6,7},{8,9},{9,10},{10,11},{11... | collective-permute-start | bytes 393224 | tf_op jit(solution)/shard_map/ppermute | solution.py:19
  132.5 1.9 %collective-permute-start.9 = (f32[8,16,2,128]{3,1,0,2:T(8,128)S(1)}, f32[8,16,2,128]{3,1,0,2:T(8,128)S(1)}, u32[]{:S(2)}, u32[]{:S(2)}) collective-permute-start(f32[8,16,2,128]{3,1,0,2:T(8,128)S(1)} %get-tuple-element.68), channel_id=1, source_target_pairs={{1,0},{2,1},{3,2},{4,3},{5,4},{6,5},{7,6},{9,8},{10,9},{11,10},{12... | collective-permute-start | bytes 393224 | tf_op jit(solution)/shard_map/ppermute | solution.py:20
  134.5 4.3 %collective-permute-done.9 = f32[8,16,2,128]{3,1,0,2:T(8,128)S(1)} collective-permute-done((f32[8,16,2,128]{3,1,0,2:T(8,128)S(1)}, f32[8,16,2,128]{3,1,0,2:T(8,128)S(1)}, u32[]{:S(2)}, u32[]{:S(2)}) %collective-permute-start.9) | collective-permute-done | bytes 131104 | tf_op jit(solution)/shard_map/ppermute | solution.py:20
  139.8 0.9 copy.20
  (59 shorter events, 5.7 us)
Async XLA Ops:
  6.5 8.4 %copy-start.3 = (f32[8,16,4,128]{3,2,1,0:T(4,128)S(1)}, f32[8,16,4,128]{3,2,1,0:T(4,128)}, u32[]{:S(2)}) copy-start(f32[8,16,4,128]{3,2,1,0:T(4,128)} %param.10) | copy-start | bytes 786436
  6.5 73.3 %all-reduce.8.cloned.1.call-start = ((), (), s32[]{:S(2)}) async-start(), calls=%async_computation | async-start | bytes 2097152 | tf_op jit(solution)/shard_map/psum | solution.py:130
  7.7 7.2 %collective-permute-start = (f32[8,16,3,128]{3,1,0,2:T(8,128)S(1)}, f32[8,16,3,128]{3,1,0,2:T(8,128)S(1)}, u32[]{:S(2)}, u32[]{:S(2)}) collective-permute-start(f32[8,16,3,128]{3,1,0,2:T(8,128)S(1)} %copy.30), channel_id=1, source_target_pairs={{0,1},{1,2},{2,3},{3,4},{4,5},{5,6},{6,7},{8,9},{9,10},{10,11},{11... | collective-permute-start | bytes 589832 | tf_op jit(solution)/shard_map/ppermute | solution.py:19
  12.4 7.0 %collective-permute-start.1 = (f32[8,16,3,128]{3,1,0,2:T(8,128)S(1)}, f32[8,16,3,128]{3,1,0,2:T(8,128)S(1)}, u32[]{:S(2)}, u32[]{:S(2)}) collective-permute-start(f32[8,16,3,128]{3,1,0,2:T(8,128)S(1)} %copy.31), channel_id=1, source_target_pairs={{1,0},{2,1},{3,2},{4,3},{5,4},{6,5},{7,6},{9,8},{10,9},{11,10},{12... | collective-permute-start | bytes 589832 | tf_op jit(solution)/shard_map/ppermute | solution.py:20
  21.8 3.5 %copy-start.1 = (bf16[8,2,16,16,512]{4,3,2,1,0:T(8,128)(2,1)S(1)}, bf16[8,2,16,16,512]{4,3,2,1,0:T(8,128)(2,1)}, u32[]{:S(2)}) copy-start(bf16[8,2,16,16,512]{4,3,2,1,0:T(8,128)(2,1)} %param.11) | copy-start | bytes 12582916
  26.5 60.6 %copy-start.4 = (s32[1024]{0:T(1024)S(1)}, s32[1024]{0:T(1024)}, u32[]{:S(2)}) copy-start(s32[1024]{0:T(1024)} %param.12) | copy-start | bytes 12292
  26.5 60.6 %copy-start.7 = (s32[1024]{0:T(1024)S(1)}, s32[1024]{0:T(1024)}, u32[]{:S(2)}) copy-start(s32[1024]{0:T(1024)} %param.13) | copy-start | bytes 12292
  81.1 6.0 %collective-permute-start.2 = (f32[2,16,1,512]{3,2,1,0:T(1,128)S(1)}, f32[2,16,1,512]{3,2,1,0:T(1,128)S(1)}, u32[]{:S(2)}, u32[]{:S(2)}) collective-permute-start(f32[2,16,1,512]{3,2,1,0:T(1,128)S(1)} %get-tuple-element.44), channel_id=1, source_target_pairs={{0,1},{1,2},{2,3},{3,4},{4,5},{5,6},{6,7},{8,9},{9,10},{10,11},{11... | collective-permute-start | bytes 196616 | tf_op jit(solution)/shard_map/ppermute | solution.py:19
  85.0 5.6 %collective-permute-start.3 = (f32[2,16,1,512]{3,2,1,0:T(1,128)S(1)}, f32[2,16,1,512]{3,2,1,0:T(1,128)S(1)}, u32[]{:S(2)}, u32[]{:S(2)}) collective-permute-start(f32[2,16,1,512]{3,2,1,0:T(1,128)S(1)} %get-tuple-element.45), channel_id=1, source_target_pairs={{1,0},{2,1},{3,2},{4,3},{5,4},{6,5},{7,6},{9,8},{10,9},{11,10},{12... | collective-permute-start | bytes 196616 | tf_op jit(solution)/shard_map/ppermute | solution.py:20
  92.9 1.2 copy-start
  95.1 3.7 %copy-start.5 = (f32[1024]{0:T(1024)S(1)}, f32[1024]{0:T(1024)}, u32[]{:S(2)}) copy-start(f32[1024]{0:T(1024)} %param.15) | copy-start | bytes 12292
  95.1 3.7 %copy-start.6 = (f32[1024]{0:T(1024)S(1)}, f32[1024]{0:T(1024)}, u32[]{:S(2)}) copy-start(f32[1024]{0:T(1024)} %param.14) | copy-start | bytes 12292
  103.7 4.6 %collective-permute-start.4 = (f32[3,16,1,512]{3,2,1,0:T(1,128)S(1)}, f32[3,16,1,512]{3,2,1,0:T(1,128)S(1)}, u32[]{:S(2)}, u32[]{:S(2)}) collective-permute-start(f32[3,16,1,512]{3,2,1,0:T(1,128)S(1)} %get-tuple-element.40), channel_id=1, source_target_pairs={{0,1},{1,2},{2,3},{3,4},{4,5},{5,6},{6,7},{8,9},{9,10},{10,11},{11... | collective-permute-start | bytes 294920 | tf_op jit(solution)/shard_map/ppermute | solution.py:19
  105.6 5.9 %collective-permute-start.5 = (f32[3,16,1,512]{3,2,1,0:T(1,128)S(1)}, f32[3,16,1,512]{3,2,1,0:T(1,128)S(1)}, u32[]{:S(2)}, u32[]{:S(2)}) collective-permute-start(f32[3,16,1,512]{3,2,1,0:T(1,128)S(1)} %get-tuple-element.41), channel_id=1, source_target_pairs={{1,0},{2,1},{3,2},{4,3},{5,4},{6,5},{7,6},{9,8},{10,9},{11,10},{12... | collective-permute-start | bytes 294920 | tf_op jit(solution)/shard_map/ppermute | solution.py:20
  113.3 2.2 %copy-start.2 = (bf16[8,2,16,16,512]{4,3,2,1,0:T(8,128)(2,1)S(1)}, bf16[8,2,16,16,512]{4,3,2,1,0:T(8,128)(2,1)}, u32[]{:S(2)}) copy-start(bf16[8,2,16,16,512]{4,3,2,1,0:T(8,128)(2,1)} %param.11) | copy-start | bytes 12582916
  121.2 5.7 %collective-permute-start.6 = (f32[8,16,128]{2,1,0:T(8,128)S(1)}, f32[8,16,128]{2,1,0:T(8,128)S(1)}, u32[]{:S(2)}, u32[]{:S(2)}) collective-permute-start(f32[8,16,128]{2,1,0:T(8,128)S(1)} %bitcast.76), channel_id=1, source_target_pairs={{1,0},{2,1},{3,2},{4,3},{5,4},{6,5},{7,6},{9,8},{10,9},{11,10},{12... | collective-permute-start | bytes 196616 | tf_op jit(solution)/shard_map/ppermute | solution.py:28
  123.2 5.0 %collective-permute-start.7 = (f32[8,16,128]{2,1,0:T(8,128)S(1)}, f32[8,16,128]{2,1,0:T(8,128)S(1)}, u32[]{:S(2)}, u32[]{:S(2)}) collective-permute-start(f32[8,16,128]{2,1,0:T(8,128)S(1)} %bitcast.75), channel_id=1, source_target_pairs={{0,1},{1,2},{2,3},{3,4},{4,5},{5,6},{6,7},{8,9},{9,10},{10,11},{11... | collective-permute-start | bytes 196616 | tf_op jit(solution)/shard_map/ppermute | solution.py:28
  128.2 6.2 %collective-permute-start.8 = (f32[8,16,2,128]{3,1,0,2:T(8,128)S(1)}, f32[8,16,2,128]{3,1,0,2:T(8,128)S(1)}, u32[]{:S(2)}, u32[]{:S(2)}) collective-permute-start(f32[8,16,2,128]{3,1,0,2:T(8,128)S(1)} %get-tuple-element.67), channel_id=1, source_target_pairs={{0,1},{1,2},{2,3},{3,4},{4,5},{5,6},{6,7},{8,9},{9,10},{10,11},{11... | collective-permute-start | bytes 393224 | tf_op jit(solution)/shard_map/ppermute | solution.py:19
  132.5 6.3 %collective-permute-start.9 = (f32[8,16,2,128]{3,1,0,2:T(8,128)S(1)}, f32[8,16,2,128]{3,1,0,2:T(8,128)S(1)}, u32[]{:S(2)}, u32[]{:S(2)}) collective-permute-start(f32[8,16,2,128]{3,1,0,2:T(8,128)S(1)} %get-tuple-element.68), channel_id=1, source_target_pairs={{1,0},{2,1},{3,2},{4,3},{5,4},{6,5},{7,6},{9,8},{10,9},{11,10},{12... | collective-permute-start | bytes 393224 | tf_op jit(solution)/shard_map/ppermute | solution.py:20
Sparse Core Ops, SparseCore 0:
  27.8 52.0 all-reduce.7
where the time goes:
time: 148 us; the launch traced here: 147 us
  waiting for transfers between devices  69.5 us (47%)
  starting transfers between devices  28.7 us (19%)
  matrix products  16.9 us (11%)
  between operations  13.9 us (9%)
  other arithmetic  11.1 us (8%)
  local copies, waits for them, and re-layouts  7.37 us (5%)
    psum x1, waiting for transfers between devices, local(): whole = lax.psum(partial_value, 'mem')  52.2 us
    ppermute x4, waiting for transfers between devices, padded_2(): after = lax.ppermute(first, axis, down)  15.4 us
    ppermute x4, starting transfers between devices, padded_2(): before = lax.ppermute(last, axis, up)  14.6 us
    ppermute x4, starting transfers between devices, padded_2(): after = lax.ppermute(first, axis, down)  8.57 us
    ppermute x2, starting transfers between devices, from_behind(): return lax.ppermute(value, axis, pairs)  5.56 us
    dot_general x1, matrix products, observe(): lax.dot_general(line_hot, weighted, (((0,), (0,)), ((), ())), precision=h...  4.19 us
    concatenate x3, other arithmetic, padded_2(): value = jnp.concatenate([before, value, after], axis=dim)  3.91 us
    dot_general x1, matrix products, observe(): jnp.dot(line_hot, table, precision=highest, preferred_element_type=jnp.fl...  3.66 us
  transfers between devices with their start and end apart: 11, of which 7 were waited for; matrix products, arithmetic and copies ran while one was open for 0% of the time, Pallas kernels for 0%

commit v1 on v0

--- a/solution.py
+++ b/solution.py
@@ -127,7 +127,9 @@
     part = jnp.einsum("ia,mlab->mlib", rows_x, smoothed, precision=highest)
     fine = jnp.einsum("mlib,jb->mlij", part, rows_y, precision=highest)
     partial_value = jnp.sum(fine[:, None] * perturbation.astype(jnp.float32), axis=0) * scale
-    whole = lax.psum(partial_value, "mem")
+    whole = partial_value
+    for hop in (1, 2):
+        whole = whole + lax.ppermute(whole, "mem", [(dev, dev ^ hop) for dev in range(4)])
     level_first = 0
     extended = jnp.pad(padded_2(whole, (("reg", 2),), 1), ((0, 0), (0, 0), (0, 0), (1, 1)))
 

time: 148 us -> 127 us (0.86)
  between operations: 13.9 us -> 0.56 us
  waiting for transfers between devices: 69.5 us -> 59.4 us
  starting transfers between devices: 28.7 us -> 35.6 us
  local copies, waits for them, and re-layouts: 7.37 us -> 4.5 us
  other arithmetic: 11.1 us -> 9.37 us
    psum x1 -> x0, waiting for transfers between devices: 52.2 us -> none  [local(): whole = lax.psum(partial_value, 'mem')]
    ppermute x0 -> x2, waiting for transfers between devices: none -> 42.1 us  [local(): lax.ppermute(whole, 'mem', [(dev, dev ^ hop) for dev in range(4)])]
    ppermute x4, starting transfers between devices: 14.6 us -> 18.9 us  [padded_2(): before = lax.ppermute(last, axis, up)]
    ppermute x0 -> x2, starting transfers between devices: none -> 2.58 us  [local(): lax.ppermute(whole, 'mem', [(dev, dev ^ hop) for dev in range(4)])]
    unnamed x21 -> x17, local copies, waits for them, and re-layouts: 1.8 us -> 0.12 us
  transfers between devices with their start and end apart: 11 -> 12, of which waited for: 7 -> 8; matrix products, arithmetic and copies ran while one was open for 0% -> 0% of each run, Pallas kernels for 0% -> 0%
where the time goes in v1:
time: 127 us; the launch traced here: 126 us
  waiting for transfers between devices  59.4 us (47%)
  starting transfers between devices  35.6 us (28%)
  matrix products  16.9 us (13%)
  other arithmetic  9.37 us (7%)
  local copies, waits for them, and re-layouts  4.5 us (4%)
    ppermute x2, waiting for transfers between devices, local(): lax.ppermute(whole, 'mem', [(dev, dev ^ hop) for dev in range(4)])  42.1 us
    ppermute x4, starting transfers between devices, padded_2(): before = lax.ppermute(last, axis, up)  18.9 us
    ppermute x4, waiting for transfers between devices, padded_2(): after = lax.ppermute(first, axis, down)  15.4 us
    ppermute x4, starting transfers between devices, padded_2(): after = lax.ppermute(first, axis, down)  8.57 us
    ppermute x2, starting transfers between devices, from_behind(): return lax.ppermute(value, axis, pairs)  5.56 us
    dot_general x1, matrix products, observe(): lax.dot_general(line_hot, weighted, (((0,), (0,)), ((), ())), precision=h...  4.19 us
    dot_general x1, matrix products, observe(): jnp.dot(line_hot, table, precision=highest, preferred_element_type=jnp.fl...  3.66 us
    dot_general x1, matrix products, local(): jnp.einsum('mlij,jb->mlib', product, rows_y, precision=highest)  3.6 us
  transfers between devices with their start and end apart: 12, of which 8 were waited for; matrix products, arithmetic and copies ran while one was open for 0% of the time, Pallas kernels for 0%

profile of v1, /device:TPU:1, one launch (start us, length us, event | category | flops | bytes accessed | tf_op | source)
XLA Modules:
  0.0 126.2 jit_solution(4367754421818866147)
XLA Ops:
  0.0 1.2 fusion.91
  1.2 4.6 %collective-permute-start = (f32[8,16,3,128]{3,1,0,2:T(8,128)S(1)}, f32[8,16,3,128]{3,1,0,2:T(8,128)S(1)}, u32[]{:S(2)}, u32[]{:S(2)}) collective-permute-start(f32[8,16,3,128]{3,1,0,2:T(8,128)S(1)} %copy.30), channel_id=1, source_target_pairs={{0,1},{1,2},{2,3},{3,4},{4,5},{5,6},{6,7},{8,9},{9,10},{10,11},{11... | collective-permute-start | bytes 589832 | tf_op jit(solution)/shard_map/ppermute | solution.py:19
  5.8 1.9 %collective-permute-start.1 = (f32[8,16,3,128]{3,1,0,2:T(8,128)S(1)}, f32[8,16,3,128]{3,1,0,2:T(8,128)S(1)}, u32[]{:S(2)}, u32[]{:S(2)}) collective-permute-start(f32[8,16,3,128]{3,1,0,2:T(8,128)S(1)} %copy.31), channel_id=1, source_target_pairs={{1,0},{2,1},{3,2},{4,3},{5,4},{6,5},{7,6},{9,8},{10,9},{11,10},{12... | collective-permute-start | bytes 589832 | tf_op jit(solution)/shard_map/ppermute | solution.py:20
  8.4 4.4 %collective-permute-done.1 = f32[8,16,3,128]{3,1,0,2:T(8,128)S(1)} collective-permute-done((f32[8,16,3,128]{3,1,0,2:T(8,128)S(1)}, f32[8,16,3,128]{3,1,0,2:T(8,128)S(1)}, u32[]{:S(2)}, u32[]{:S(2)}) %collective-permute-start.1) | collective-permute-done | bytes 196640 | tf_op jit(solution)/shard_map/ppermute | solution.py:20
  14.1 1.2 convolution_bitcast_fusion
  15.3 3.5 %fusion.49 = f32[8,16,16,512]{3,2,1,0:T(8,128)S(1)} fusion(f32[8,16,16,128]{3,2,1,0:T(8,128)S(1)} %convolution_bitcast_fusion, f32[128]{0:T(128)S(1)} %iota_convert_fusion, f32[512]{0:T(512)S(1)} %multiply_add_fusion), kind=kOutput, calls=%fused_computation.114 | convolution fusion | flops 1610874880 | bytes 5245440 | tf_op jit(solution)/shard_map/mlib,jb->mlij/dot_general | solution.py:128
  18.8 1.1 fusion
  20.1 1.3 %collective-permute-start.2 = (f32[2,16,16,512]{3,2,1,0:T(8,128)S(1)}, f32[2,16,16,512]{3,2,1,0:T(8,128)S(1)}, u32[]{:S(2)}, u32[]{:S(2)}) collective-permute-start(f32[2,16,16,512]{3,2,1,0:T(8,128)S(1)} %broadcast_multiply_fusion), channel_id=1, source_target_pairs={{0,8},{8,0},{16,24},{24,16},{1,9},{9,1},{17,25},{25,17},{2,10},{10... | collective-permute-start | bytes 3145736 | tf_op jit(solution)/shard_map/ppermute | solution.py:132
  21.4 20.5 %collective-permute-done.2 = f32[2,16,16,512]{3,2,1,0:T(8,128)S(1)} collective-permute-done((f32[2,16,16,512]{3,2,1,0:T(8,128)S(1)}, f32[2,16,16,512]{3,2,1,0:T(8,128)S(1)}, u32[]{:S(2)}, u32[]{:S(2)}) %collective-permute-start.2) | collective-permute-done | bytes 1048608 | tf_op jit(solution)/shard_map/ppermute | solution.py:132
  42.2 1.3 %collective-permute-start.3 = (f32[2,16,16,512]{3,2,1,0:T(8,128)S(1)}, f32[2,16,16,512]{3,2,1,0:T(8,128)S(1)}, u32[]{:S(2)}, u32[]{:S(2)}) collective-permute-start(f32[2,16,16,512]{3,2,1,0:T(8,128)S(1)} %fusion.86), channel_id=1, source_target_pairs={{0,16},{8,24},{16,0},{24,8},{1,17},{9,25},{17,1},{25,9},{2,18},{10... | collective-permute-start | bytes 3145736 | tf_op jit(solution)/shard_map/ppermute | solution.py:132
  43.5 21.6 %collective-permute-done.3 = f32[2,16,16,512]{3,2,1,0:T(8,128)S(1)} collective-permute-done((f32[2,16,16,512]{3,2,1,0:T(8,128)S(1)}, f32[2,16,16,512]{3,2,1,0:T(8,128)S(1)}, u32[]{:S(2)}, u32[]{:S(2)}) %collective-permute-start.3) | collective-permute-done | bytes 1048608 | tf_op jit(solution)/shard_map/ppermute | solution.py:132
  65.5 8.1 %collective-permute-start.4 = (f32[2,16,1,512]{3,2,1,0:T(1,128)S(1)}, f32[2,16,1,512]{3,2,1,0:T(1,128)S(1)}, u32[]{:S(2)}, u32[]{:S(2)}) collective-permute-start(f32[2,16,1,512]{3,2,1,0:T(1,128)S(1)} %get-tuple-element.44), channel_id=1, source_target_pairs={{0,1},{1,2},{2,3},{3,4},{4,5},{5,6},{6,7},{8,9},{9,10},{10,11},{11... | collective-permute-start | bytes 196616 | tf_op jit(solution)/shard_map/ppermute | solution.py:19
  73.6 2.1 %collective-permute-start.5 = (f32[2,16,1,512]{3,2,1,0:T(1,128)S(1)}, f32[2,16,1,512]{3,2,1,0:T(1,128)S(1)}, u32[]{:S(2)}, u32[]{:S(2)}) collective-permute-start(f32[2,16,1,512]{3,2,1,0:T(1,128)S(1)} %get-tuple-element.45), channel_id=1, source_target_pairs={{1,0},{2,1},{3,2},{4,3},{5,4},{6,5},{7,6},{9,8},{10,9},{11,10},{12... | collective-permute-start | bytes 196616 | tf_op jit(solution)/shard_map/ppermute | solution.py:20
  75.8 3.4 %collective-permute-done.5 = f32[2,16,1,512]{3,2,1,0:T(1,128)S(1)} collective-permute-done((f32[2,16,1,512]{3,2,1,0:T(1,128)S(1)}, f32[2,16,1,512]{3,2,1,0:T(1,128)S(1)}, u32[]{:S(2)}, u32[]{:S(2)}) %collective-permute-start.5) | collective-permute-done | bytes 65568 | tf_op jit(solution)/shard_map/ppermute | solution.py:20
  79.2 1.1 select_maximum_fusion.4
  80.4 0.8 fusion.27
  81.4 3.7 %select_reduce_fusion = f32[1024]{0:T(1024)S(1)} fusion(f32[1024,512]{1,0:T(8,128)S(1)} %bitcast.71, s32[1024]{0:T(1024)S(1)} %get-tuple-element.72, s32[1024]{0:T(1024)S(1)} %get-tuple-element.71), kind=kOutput, calls=%fused_computation.30 | convolution fusion | flops 6445071360 | bytes 2109440 | tf_op jit(solution)/shard_map/dot_general | solution.py:98
  85.1 4.2 %fusion.2 = f32[1024,512]{1,0:T(8,128)S(1)} fusion(s32[1024]{0:T(1024)S(1)} %get-tuple-element.72, f32[1024]{0:T(1024)S(1)} %multiply_select_fusion, s32[1024]{0:T(1024)S(1)} %get-tuple-element.71), kind=kOutput, calls=%fused_computation.7 | convolution fusion | flops 6444548096 | bytes 2109440 | tf_op jit(solution)/shard_map/dot_general | solution.py:102
  89.9 1.9 %collective-permute-start.6 = (f32[3,16,1,512]{3,2,1,0:T(1,128)S(1)}, f32[3,16,1,512]{3,2,1,0:T(1,128)S(1)}, u32[]{:S(2)}, u32[]{:S(2)}) collective-permute-start(f32[3,16,1,512]{3,2,1,0:T(1,128)S(1)} %get-tuple-element.40), channel_id=1, source_target_pairs={{0,1},{1,2},{2,3},{3,4},{4,5},{5,6},{6,7},{8,9},{9,10},{10,11},{11... | collective-permute-start | bytes 294920 | tf_op jit(solution)/shard_map/ppermute | solution.py:19
  91.8 2.6 %collective-permute-start.7 = (f32[3,16,1,512]{3,2,1,0:T(1,128)S(1)}, f32[3,16,1,512]{3,2,1,0:T(1,128)S(1)}, u32[]{:S(2)}, u32[]{:S(2)}) collective-permute-start(f32[3,16,1,512]{3,2,1,0:T(1,128)S(1)} %get-tuple-element.41), channel_id=1, source_target_pairs={{1,0},{2,1},{3,2},{4,3},{5,4},{6,5},{7,6},{9,8},{10,9},{11,10},{12... | collective-permute-start | bytes 294920 | tf_op jit(solution)/shard_map/ppermute | solution.py:20
  94.4 3.3 %collective-permute-done.7 = f32[3,16,1,512]{3,2,1,0:T(1,128)S(1)} collective-permute-done((f32[3,16,1,512]{3,2,1,0:T(1,128)S(1)}, f32[3,16,1,512]{3,2,1,0:T(1,128)S(1)}, u32[]{:S(2)}, u32[]{:S(2)}) %collective-permute-start.7) | collective-permute-done | bytes 98336 | tf_op jit(solution)/shard_map/ppermute | solution.py:20
  97.7 1.6 %select_maximum_fusion = f32[3,16,18,514]{3,2,1,0:T(8,128)S(1)} fusion(f32[3,16,1,512]{3,2,1,0:T(1,128)S(1)} %collective-permute-done.7, f32[3,16,1,512]{3,2,1,0:T(1,128)S(1)} %collective-permute-done.6, f32[1,16,16,512]{3,2,1,0:T(8,128)S(1)} %get-tuple-element.43, f32[1,16,16,512]{3,2,1,0:T(8,128)S(1)} %get-tuple-element.42, f32[1,16,16,512]{3,2,1,0:T(8,128)S(1)} %bitcast.70), kind=kLoop, calls=%fused_computation.9 | loop fusion | flops 5329152 | bytes 3545856 | tf_op jit(solution)/shard_map/concatenate | solution.py:21
  99.5 1.5 %fusion.18 = (f32[1,16,16,512]{3,2,1,0:T(8,128)S(1)}, f32[1,16,16,512]{3,2,1,0:T(8,128)S(1)}) fusion(f32[16,18,514]{2,1,0:T(8,128)S(1)} %get-tuple-element.31, f32[16,18,514]{2,1,0:T(8,128)S(1)} %get-tuple-element.29, f32[16,18,514]{2,1,0:T(8,128)S(1)} %get-tuple-element.30, f32[16,16,512]{2,1,0:T(8,128)S(1)} %bitcast.72, f32[16,16,512]{2,1,0:T(8,128)S(1)} %bitcast.68, ...), kind=kLoop, calls=%fused_computation.60 | loop fusion | flops 2621440 | bytes 8912896 | tf_op jit(solution)/shard_map/stack | solution.py:116
  101.1 1.2 fusion.1
  102.3 3.6 %fusion.47 = f32[8,16,16,128]{3,2,1,0:T(8,128)S(1)} fusion(f32[8,16,16,512]{3,2,1,0:T(8,128)S(1)} %fusion.1, f32[128]{0:T(128)S(1)} %iota_convert_fusion, f32[512]{0:T(512)S(1)} %multiply_add_fusion), kind=kOutput, calls=%fused_computation.112 | convolution fusion | flops 1610874880 | bytes 5245440 | tf_op jit(solution)/shard_map/mlij,jb->mlib/dot_general | solution.py:142
  106.8 1.9 %collective-permute-start.8 = (f32[8,16,128]{2,1,0:T(8,128)S(1)}, f32[8,16,128]{2,1,0:T(8,128)S(1)}, u32[]{:S(2)}, u32[]{:S(2)}) collective-permute-start(f32[8,16,128]{2,1,0:T(8,128)S(1)} %bitcast.76), channel_id=1, source_target_pairs={{1,0},{2,1},{3,2},{4,3},{5,4},{6,5},{7,6},{9,8},{10,9},{11,10},{12... | collective-permute-start | bytes 196616 | tf_op jit(solution)/shard_map/ppermute | solution.py:28
  108.8 3.6 %collective-permute-start.9 = (f32[8,16,128]{2,1,0:T(8,128)S(1)}, f32[8,16,128]{2,1,0:T(8,128)S(1)}, u32[]{:S(2)}, u32[]{:S(2)}) collective-permute-start(f32[8,16,128]{2,1,0:T(8,128)S(1)} %bitcast.75), channel_id=1, source_target_pairs={{0,1},{1,2},{2,3},{3,4},{4,5},{5,6},{6,7},{8,9},{9,10},{10,11},{11... | collective-permute-start | bytes 196616 | tf_op jit(solution)/shard_map/ppermute | solution.py:28
  112.5 1.3 %collective-permute-done.9 = f32[8,16,128]{2,1,0:T(8,128)S(1)} collective-permute-done((f32[8,16,128]{2,1,0:T(8,128)S(1)}, f32[8,16,128]{2,1,0:T(8,128)S(1)}, u32[]{:S(2)}, u32[]{:S(2)}) %collective-permute-start.9) | collective-permute-done | bytes 65568 | tf_op jit(solution)/shard_map/ppermute | solution.py:28
  113.8 4.3 %collective-permute-start.10 = (f32[8,16,2,128]{3,1,0,2:T(8,128)S(1)}, f32[8,16,2,128]{3,1,0,2:T(8,128)S(1)}, u32[]{:S(2)}, u32[]{:S(2)}) collective-permute-start(f32[8,16,2,128]{3,1,0,2:T(8,128)S(1)} %get-tuple-element.67), channel_id=1, source_target_pairs={{0,1},{1,2},{2,3},{3,4},{4,5},{5,6},{6,7},{8,9},{9,10},{10,11},{11... | collective-permute-start | bytes 393224 | tf_op jit(solution)/shard_map/ppermute | solution.py:19
  118.1 1.9 %collective-permute-start.11 = (f32[8,16,2,128]{3,1,0,2:T(8,128)S(1)}, f32[8,16,2,128]{3,1,0,2:T(8,128)S(1)}, u32[]{:S(2)}, u32[]{:S(2)}) collective-permute-start(f32[8,16,2,128]{3,1,0,2:T(8,128)S(1)} %get-tuple-element.68), channel_id=1, source_target_pairs={{1,0},{2,1},{3,2},{4,3},{5,4},{6,5},{7,6},{9,8},{10,9},{11,10},{12... | collective-permute-start | bytes 393224 | tf_op jit(solution)/shard_map/ppermute | solution.py:20
  120.0 4.3 %collective-permute-done.11 = f32[8,16,2,128]{3,1,0,2:T(8,128)S(1)} collective-permute-done((f32[8,16,2,128]{3,1,0,2:T(8,128)S(1)}, f32[8,16,2,128]{3,1,0,2:T(8,128)S(1)}, u32[]{:S(2)}, u32[]{:S(2)}) %collective-permute-start.11) | collective-permute-done | bytes 131104 | tf_op jit(solution)/shard_map/ppermute | solution.py:20
  125.4 0.9 copy.20
  (58 shorter events, 5.8 us)
Async XLA Ops:
  0.0 8.4 %copy-start.1 = (f32[8,16,4,128]{3,2,1,0:T(4,128)S(1)}, f32[8,16,4,128]{3,2,1,0:T(4,128)}, u32[]{:S(2)}) copy-start(f32[8,16,4,128]{3,2,1,0:T(4,128)} %param.10) | copy-start | bytes 786436
  1.2 7.2 %collective-permute-start = (f32[8,16,3,128]{3,1,0,2:T(8,128)S(1)}, f32[8,16,3,128]{3,1,0,2:T(8,128)S(1)}, u32[]{:S(2)}, u32[]{:S(2)}) collective-permute-start(f32[8,16,3,128]{3,1,0,2:T(8,128)S(1)} %copy.30), channel_id=1, source_target_pairs={{0,1},{1,2},{2,3},{3,4},{4,5},{5,6},{6,7},{8,9},{9,10},{10,11},{11... | collective-permute-start | bytes 589832 | tf_op jit(solution)/shard_map/ppermute | solution.py:19
  5.8 7.0 %collective-permute-start.1 = (f32[8,16,3,128]{3,1,0,2:T(8,128)S(1)}, f32[8,16,3,128]{3,1,0,2:T(8,128)S(1)}, u32[]{:S(2)}, u32[]{:S(2)}) collective-permute-start(f32[8,16,3,128]{3,1,0,2:T(8,128)S(1)} %copy.31), channel_id=1, source_target_pairs={{1,0},{2,1},{3,2},{4,3},{5,4},{6,5},{7,6},{9,8},{10,9},{11,10},{12... | collective-permute-start | bytes 589832 | tf_op jit(solution)/shard_map/ppermute | solution.py:20
  15.3 3.5 %copy-start = (bf16[8,2,16,16,512]{4,3,2,1,0:T(8,128)(2,1)S(1)}, bf16[8,2,16,16,512]{4,3,2,1,0:T(8,128)(2,1)}, u32[]{:S(2)}) copy-start(bf16[8,2,16,16,512]{4,3,2,1,0:T(8,128)(2,1)} %param.11) | copy-start | bytes 12582916
  20.1 21.8 %collective-permute-start.2 = (f32[2,16,16,512]{3,2,1,0:T(8,128)S(1)}, f32[2,16,16,512]{3,2,1,0:T(8,128)S(1)}, u32[]{:S(2)}, u32[]{:S(2)}) collective-permute-start(f32[2,16,16,512]{3,2,1,0:T(8,128)S(1)} %broadcast_multiply_fusion), channel_id=1, source_target_pairs={{0,8},{8,0},{16,24},{24,16},{1,9},{9,1},{17,25},{25,17},{2,10},{10... | collective-permute-start | bytes 3145736 | tf_op jit(solution)/shard_map/ppermute | solution.py:132
  42.2 33.5 %copy-start.2 = (s32[1024]{0:T(1024)S(1)}, s32[1024]{0:T(1024)}, u32[]{:S(2)}) copy-start(s32[1024]{0:T(1024)} %param.12) | copy-start | bytes 12292
  42.2 33.5 %copy-start.5 = (s32[1024]{0:T(1024)S(1)}, s32[1024]{0:T(1024)}, u32[]{:S(2)}) copy-start(s32[1024]{0:T(1024)} %param.13) | copy-start | bytes 12292
  42.2 22.9 %collective-permute-start.3 = (f32[2,16,16,512]{3,2,1,0:T(8,128)S(1)}, f32[2,16,16,512]{3,2,1,0:T(8,128)S(1)}, u32[]{:S(2)}, u32[]{:S(2)}) collective-permute-start(f32[2,16,16,512]{3,2,1,0:T(8,128)S(1)} %fusion.86), channel_id=1, source_target_pairs={{0,16},{8,24},{16,0},{24,8},{1,17},{9,25},{17,1},{25,9},{2,18},{10... | collective-permute-start | bytes 3145736 | tf_op jit(solution)/shard_map/ppermute | solution.py:132
  65.5 10.3 %collective-permute-start.4 = (f32[2,16,1,512]{3,2,1,0:T(1,128)S(1)}, f32[2,16,1,512]{3,2,1,0:T(1,128)S(1)}, u32[]{:S(2)}, u32[]{:S(2)}) collective-permute-start(f32[2,16,1,512]{3,2,1,0:T(1,128)S(1)} %get-tuple-element.44), channel_id=1, source_target_pairs={{0,1},{1,2},{2,3},{3,4},{4,5},{5,6},{6,7},{8,9},{9,10},{10,11},{11... | collective-permute-start | bytes 196616 | tf_op jit(solution)/shard_map/ppermute | solution.py:19
  73.6 5.6 %collective-permute-start.5 = (f32[2,16,1,512]{3,2,1,0:T(1,128)S(1)}, f32[2,16,1,512]{3,2,1,0:T(1,128)S(1)}, u32[]{:S(2)}, u32[]{:S(2)}) collective-permute-start(f32[2,16,1,512]{3,2,1,0:T(1,128)S(1)} %get-tuple-element.45), channel_id=1, source_target_pairs={{1,0},{2,1},{3,2},{4,3},{5,4},{6,5},{7,6},{9,8},{10,9},{11,10},{12... | collective-permute-start | bytes 196616 | tf_op jit(solution)/shard_map/ppermute | solution.py:20
  81.4 3.7 %copy-start.3 = (f32[1024]{0:T(1024)S(1)}, f32[1024]{0:T(1024)}, u32[]{:S(2)}) copy-start(f32[1024]{0:T(1024)} %param.15) | copy-start | bytes 12292
  81.4 3.7 %copy-start.4 = (f32[1024]{0:T(1024)S(1)}, f32[1024]{0:T(1024)}, u32[]{:S(2)}) copy-start(f32[1024]{0:T(1024)} %param.14) | copy-start | bytes 12292
  89.9 4.6 %collective-permute-start.6 = (f32[3,16,1,512]{3,2,1,0:T(1,128)S(1)}, f32[3,16,1,512]{3,2,1,0:T(1,128)S(1)}, u32[]{:S(2)}, u32[]{:S(2)}) collective-permute-start(f32[3,16,1,512]{3,2,1,0:T(1,128)S(1)} %get-tuple-element.40), channel_id=1, source_target_pairs={{0,1},{1,2},{2,3},{3,4},{4,5},{5,6},{6,7},{8,9},{9,10},{10,11},{11... | collective-permute-start | bytes 294920 | tf_op jit(solution)/shard_map/ppermute | solution.py:19
  91.8 5.9 %collective-permute-start.7 = (f32[3,16,1,512]{3,2,1,0:T(1,128)S(1)}, f32[3,16,1,512]{3,2,1,0:T(1,128)S(1)}, u32[]{:S(2)}, u32[]{:S(2)}) collective-permute-start(f32[3,16,1,512]{3,2,1,0:T(1,128)S(1)} %get-tuple-element.41), channel_id=1, source_target_pairs={{1,0},{2,1},{3,2},{4,3},{5,4},{6,5},{7,6},{9,8},{10,9},{11,10},{12... | collective-permute-start | bytes 294920 | tf_op jit(solution)/shard_map/ppermute | solution.py:20
  106.8 5.7 %collective-permute-start.8 = (f32[8,16,128]{2,1,0:T(8,128)S(1)}, f32[8,16,128]{2,1,0:T(8,128)S(1)}, u32[]{:S(2)}, u32[]{:S(2)}) collective-permute-start(f32[8,16,128]{2,1,0:T(8,128)S(1)} %bitcast.76), channel_id=1, source_target_pairs={{1,0},{2,1},{3,2},{4,3},{5,4},{6,5},{7,6},{9,8},{10,9},{11,10},{12... | collective-permute-start | bytes 196616 | tf_op jit(solution)/shard_map/ppermute | solution.py:28
  108.8 5.0 %collective-permute-start.9 = (f32[8,16,128]{2,1,0:T(8,128)S(1)}, f32[8,16,128]{2,1,0:T(8,128)S(1)}, u32[]{:S(2)}, u32[]{:S(2)}) collective-permute-start(f32[8,16,128]{2,1,0:T(8,128)S(1)} %bitcast.75), channel_id=1, source_target_pairs={{0,1},{1,2},{2,3},{3,4},{4,5},{5,6},{6,7},{8,9},{9,10},{10,11},{11... | collective-permute-start | bytes 196616 | tf_op jit(solution)/shard_map/ppermute | solution.py:28
  113.8 6.2 %collective-permute-start.10 = (f32[8,16,2,128]{3,1,0,2:T(8,128)S(1)}, f32[8,16,2,128]{3,1,0,2:T(8,128)S(1)}, u32[]{:S(2)}, u32[]{:S(2)}) collective-permute-start(f32[8,16,2,128]{3,1,0,2:T(8,128)S(1)} %get-tuple-element.67), channel_id=1, source_target_pairs={{0,1},{1,2},{2,3},{3,4},{4,5},{5,6},{6,7},{8,9},{9,10},{10,11},{11... | collective-permute-start | bytes 393224 | tf_op jit(solution)/shard_map/ppermute | solution.py:19
  118.1 6.3 %collective-permute-start.11 = (f32[8,16,2,128]{3,1,0,2:T(8,128)S(1)}, f32[8,16,2,128]{3,1,0,2:T(8,128)S(1)}, u32[]{:S(2)}, u32[]{:S(2)}) collective-permute-start(f32[8,16,2,128]{3,1,0,2:T(8,128)S(1)} %get-tuple-element.68), channel_id=1, source_target_pairs={{1,0},{2,1},{3,2},{4,3},{5,4},{6,5},{7,6},{9,8},{10,9},{11,10},{12... | collective-permute-start | bytes 393224 | tf_op jit(solution)/shard_map/ppermute | solution.py:20
